TPU v7x, 256 devices: a whole 4x4x8 slice. The times are simulated.
256 devices in a mesh: front: 8 (over x, core), grp: 32 (over y, z).
Axes of the slice: x: 4, y: 4, z: 8, core: 2. Of those that a mesh axis runs over, the one named last changes fastest.
Arguments:
- panel_block: bfloat16 [8, 4608, 1024], P('front', 'grp'), may hold values from -0.1796875 to 0.1796875
- trailing: float32 [8, 4608, 4608], P('front', 'grp')
- inverse: float32 [8, 1024, 1024], P('front')
- weights: float32 [8, 4608], P('front'), may hold values from -0.09375 to 0.09375
- live_size: int32 [8], P('front'), may hold values from 2304 to 4608, as said below
- column_source: int32 [8, 4608], P('front'), may hold values from 0 to 4607, each once within a row
- destination: int32 [8, 4608, 1], P('front', 'grp'), may hold values from 0 to 7; in each aligned block of 144 rows (0 to 143, 144 to 287, ..., all dimensions but the last counted through in order) at most 36 rows name the same one
- row_offset: int32 [8, 4608], P('front', 'grp'), may hold values from 0 to 143
Outputs:
- factor: float32 [8, 4608, 1024], P('front', 'grp')
- checksum: float32 [8, 4608], P('front', 'grp')
- ancestor: float32 [8, 4608, 4608], P('front', 'grp')
Inputs may be any that keep to these rules, and one draw needn't show every extreme that they name: `live_size`: each front's live size is 4608 minus a multiple of 576; one front is full. `destination`: among the 144 rows of one device at most 36 rows name the same ancestor front. `column_source`: each front's row is a permutation.
All inputs are finite; a program needn't handle non-finite values.
Results may differ from a plain program's by a relative error of at most 0.0003.
Values may be sent and summed in bfloat16 or wider, within the bound.
A program may use at most 128 MiB of HBM per device.

v0:
```python
import jax
import jax.numpy as jnp
from jax import lax
from jax.sharding import PartitionSpec as P


def place_columns(rows, source, live_count):
    keep_cols = (source < live_count).astype(jnp.float32)
    return jnp.take(rows, source, axis=1) * keep_cols[None, :]


def on_device(
    panel_block, trailing, inverse, weights, live_size, column_source, destination, row_offset
):
    highest_precision = lax.Precision.HIGHEST
    row_count = trailing.shape[1]
    col_count = trailing.shape[2]
    fronts = lax.axis_size("front")
    capacity = max(2, 2 * row_count // fronts)
    trail_rows = trailing[0]
    inverse_rows = inverse[0]
    live_count = live_size[0]
    panel_f32 = panel_block[0].astype(jnp.float32)
    factor = jnp.dot(panel_f32, inverse_rows.T, precision=highest_precision)
    update = lax.dot_general(
        factor,
        lax.all_gather(factor, "grp", axis=0, tiled=True),
        (((1,), (1,)), ((), ())),
        precision=highest_precision,
        preferred_element_type=jnp.float32,
    )
    schur_rows = trail_rows - update
    positions = jnp.arange(col_count, dtype=jnp.int32)
    colmask = (positions < live_count).astype(jnp.float32)
    masked_weights = weights[0] * colmask
    checksum = jnp.dot(schur_rows, masked_weights, precision=highest_precision)
    global_rows = lax.axis_index("grp") * row_count + jnp.arange(row_count, dtype=jnp.int32)
    live_rows = global_rows < live_count
    dest_front = destination[0, :, 0]
    front_ids = jnp.arange(fronts, dtype=jnp.int32)
    onehot = ((dest_front[:, None] == front_ids[None, :]) & live_rows[:, None]).astype(jnp.int32)
    running = jnp.cumsum(onehot, axis=0)
    slot_index = jnp.sum(onehot * (running - 1), axis=1)
    dest_live = jnp.where(live_rows, dest_front, fronts)
    row_tags = (
        jnp.full((fronts, capacity), -1.0, jnp.float32)
        .at[dest_live, slot_index]
        .set(row_offset[0].astype(jnp.float32), mode="drop")
    )
    permuted = place_columns(schur_rows, column_source[0], live_count)
    bucket = (
        jnp.zeros((fronts, capacity, col_count), jnp.float32)
        .at[dest_live, slot_index]
        .set(permuted, mode="drop")
    )
    received, received_tags = (
        lax.all_to_all(bucket, "front", split_axis=0, concat_axis=0, tiled=True),
        lax.all_to_all(row_tags, "front", split_axis=0, concat_axis=0, tiled=True),
    )
    flat_rows = received.reshape(fronts * capacity, col_count)
    flat_tags = received_tags.reshape(fronts * capacity)
    target_row = jnp.where(flat_tags < 0.0, row_count, flat_tags.astype(jnp.int32))
    ancestor = (
        jnp.zeros((row_count, col_count), jnp.float32).at[target_row].add(flat_rows, mode="drop")
    )
    return (factor[None], checksum[None], ancestor[None])


def solution(mesh):
    placed = (
        P("front", "grp", None),
        P("front", "grp", None),
        P("front", None, None),
        P("front", None),
        P("front"),
        P("front", None),
        P("front", "grp", None),
        P("front", "grp"),
    )
    return jax.shard_map(
        on_device,
        mesh=mesh,
        in_specs=placed,
        out_specs=(P("front", "grp", None), P("front", "grp"), P("front", "grp", None)),
        check_vma=False,
    )
```

profile of v0, /device:TPU:1, one launch (start us, length us, event | category | flops | bytes accessed | tf_op | source)
XLA Modules:
  0.0 366.7 jit_solution(13603879904250098993)
XLA Ops:
  7.2 0.0 copy-start
  7.2 0.0 copy-start.4
  7.2 0.0 copy-start.5
  7.2 0.0 copy-start.2
  7.2 0.0 all-gather.2.cloned.1.call-start
  7.3 0.9 copy-done
  8.1 5.4 %fusion = f32[144,1024]{1,0:T(8,128)} fusion(f32[1,1024,1024]{2,1,0:T(8,128)} %param.10, bf16[1,144,1024]{2,1,0:T(8,128)(2,1)S(1)} %copy-done), kind=kOutput, calls=%fused_computation.6 | convolution fusion | flops 1811939328 | bytes 5079040 | tf_op jit(solution)/shard_map/dot_general | solution.py:24
  13.6 0.0 all-gather.2.cloned.1.call-update
  14.3 0.0 copy-done.4
  14.3 0.6 reduce-window.6
  14.9 0.2 slice_reduce_fusion
  15.1 0.0 copy-done.5
  15.1 0.1 add_bitcast_fusion
  15.3 0.6 broadcast_in_dim.49
  15.9 22.1 %scatter_fusion = f32[8,36]{1,0:T(8,128)} fusion(f32[8,36]{1,0:T(8,128)} %broadcast_in_dim.49, s32[144]{0:T(256)S(1)} %bitcast.39, f32[144]{0:T(256)S(1)} %bitcast.45), kind=kCustom, calls=%fused_computation.1 | custom fusion | bytes 2880 | tf_op jit(solution)/shard_map/scatter | solution.py:48
  37.9 6.4 %all-to-all-start = ((f32[8,1,36]{2,1,0:T(1,128)}), f32[8,1,36]{2,1,0:T(1,128)S(1)}, u32[]{:S(2)}, u32[]{:S(2)}) async-start(f32[8,1,36]{2,1,0:T(1,128)} %bitcast.15), calls=%async_computation | async-start | bytes 8192 | tf_op jit(solution)/shard_map/all_to_all | solution.py:58
  44.4 0.0 copy-done.2
  44.4 0.1 fusion.6
  44.5 0.1 fusion.7
  44.6 123.4 %all-gather.2.cloned.1.call-done = f32[4608,1024]{1,0:T(8,128)} async-done(((f32[144,1024]{1,0:T(8,128)}), f32[4608,1024]{1,0:T(8,128)}) %all-gather.2.cloned.1.call-update) | async-done | bytes 18874384 | tf_op jit(solution)/shard_map/all_gather | solution.py:27
  168.0 23.8 %convolution_subtract_fusion = f32[144,4608]{1,0:T(8,128)S(1)} fusion(f32[144,1024]{1,0:T(8,128)} %fusion, f32[4608,1024]{1,0:T(8,128)} %all-gather.2.cloned.1.call-done, f32[1,144,4608]{2,1,0:T(8,128)} %param.9), kind=kOutput, calls=%fused_computation.4 | convolution fusion | flops 8154390528 | bytes 24772608 | tf_op jit(solution)/shard_map/dot_general | solution.py:25
  191.8 3.4 copy.17
  195.2 14.1 %gather_fusion = f32[4608,144]{1,0:T(8,128)} fusion(f32[144,4608]{0,1:T(8,128)} %copy.17, s32[5120]{0:T(1024)S(1)} %pad_clamp_fusion), kind=kCustom, calls=%fused_computation | custom fusion | bytes 5326848 | tf_op jit(solution)/shard_map/jit(_take)/gather | solution.py:9
  209.3 6.4 %multiply_bitcast_fusion = f32[144,4608]{0,1:T(8,128)} fusion(f32[4608,144]{1,0:T(8,128)} %gather_fusion, f32[4608]{0:T(1024)S(1)} %fusion.7, pred[4608]{0:T(1024)(128)(4,1)S(1)} %compare_and_fusion), kind=kLoop, calls=%fused_computation.5 | loop fusion | flops 1327104 | bytes 5331456 | tf_op jit(solution)/shard_map/mul | solution.py:9
  215.7 5.3 %copy.18 = f32[144,4608]{1,0:T(8,128)} copy(f32[144,4608]{0,1:T(8,128)} %multiply_bitcast_fusion) | data formatting | bytes 5308416 | tf_op jit(solution)/shard_map/mul | solution.py:9
  221.0 3.0 broadcast_in_dim.53
  224.0 39.0 %scatter_fusion.1 = f32[8,36,4608]{2,0,1:T(8,128)} fusion(f32[8,36,4608]{2,0,1:T(8,128)} %broadcast_in_dim.53, s32[144]{0:T(256)S(1)} %bitcast.40, f32[144,4608]{1,0:T(8,128)} %copy.18), kind=kCustom, calls=%fused_computation.2 | custom fusion | bytes 7963776 | tf_op jit(solution)/shard_map/scatter | solution.py:54
  263.0 8.1 %copy.19 = f32[8,36,4608]{2,1,0:T(8,128)} copy(f32[8,36,4608]{2,0,1:T(8,128)} %scatter_fusion.1) | data formatting | bytes 10616832 | tf_op jit(solution)/shard_map/scatter | solution.py:54
  271.1 0.0 copy-start.3
  271.1 0.0 all-to-all-done
  271.1 5.4 %all-to-all-start.1 = ((f32[8,36,4608]{2,1,0:T(8,128)}), f32[8,36,4608]{2,1,0:T(8,128)}, u32[]{:S(2)}, u32[]{:S(2)}) async-start(f32[8,36,4608]{2,1,0:T(8,128)} %copy.19), calls=%async_computation.1 | async-start | bytes 11796480 | tf_op jit(solution)/shard_map/all_to_all | solution.py:57
  276.6 0.0 copy-done.3
  276.7 0.1 select_n.81
  276.8 0.0 copy-start.1
  276.8 2.7 fusion.15
  279.5 64.2 %all-to-all-done.1 = f32[8,36,4608]{2,1,0:T(8,128)} async-done(((f32[8,36,4608]{2,1,0:T(8,128)}), f32[8,36,4608]{2,1,0:T(8,128)}, u32[]{:S(2)}, u32[]{:S(2)}) %all-to-all-start.1) | async-done | bytes 5308448 | tf_op jit(solution)/shard_map/all_to_all | solution.py:57
  343.7 5.6 %reshape.169 = f32[288,4608]{1,0:T(8,128)} reshape(f32[8,36,4608]{2,1,0:T(8,128)} %all-to-all-done.1) | data formatting | bytes 10616832 | tf_op jit(solution)/shard_map/reshape | solution.py:60
  349.3 10.6 %scatter_custom_fusion.2 = f32[144,4608]{1,0:T(8,128)} fusion(s32[288]{0:T(512)S(1)} %fusion.13, f32[288,4608]{1,0:T(8,128)} %reshape.169, f32[]{:T(128)} %constant.13.clone.1), kind=kCustom, calls=%fused_computation.8 | custom fusion | flops 1327104 | bytes 2654720 | tf_op jit(solution)/shard_map/scatter-add | solution.py:64
  359.9 0.0 copy-done.1
  (16 shorter events, 0.3 us)
Async XLA Ops:
  7.2 1.0 copy-start
  7.2 7.1 %copy-start.4 = (s32[1,144,1]{1,2,0:T(1,128)S(1)}, s32[1,144,1]{1,2,0:T(1,128)}, u32[]{:S(2)}) copy-start(s32[1,144,1]{1,2,0:T(1,128)} %param.14) | copy-start | bytes 1732
  7.2 7.9 %copy-start.5 = (s32[1,144]{1,0:T(1,128)S(1)}, s32[1,144]{1,0:T(1,128)}, u32[]{:S(2)}) copy-start(s32[1,144]{1,0:T(1,128)} %param.15) | copy-start | bytes 1732
  7.2 37.2 %copy-start.2 = (s32[1,4608]{1,0:T(1,128)S(1)}, s32[1,4608]{1,0:T(1,128)}, u32[]{:S(2)}) copy-start(s32[1,4608]{1,0:T(1,128)} %param.13) | copy-start | bytes 55300
  7.2 160.8 %all-gather.2.cloned.1.call-start = ((), (), s32[]{:S(2)}) async-start(), calls=%async_computation.2 | async-start | bytes 19464192 | tf_op jit(solution)/shard_map/all_gather | solution.py:27
  37.9 233.2 %all-to-all-start = ((f32[8,1,36]{2,1,0:T(1,128)}), f32[8,1,36]{2,1,0:T(1,128)S(1)}, u32[]{:S(2)}, u32[]{:S(2)}) async-start(f32[8,1,36]{2,1,0:T(1,128)} %bitcast.15), calls=%async_computation | async-start | bytes 8192 | tf_op jit(solution)/shard_map/all_to_all | solution.py:58
  271.1 5.4 %copy-start.3 = (f32[1,4608]{1,0:T(1,128)S(1)}, f32[1,4608]{1,0:T(1,128)}, u32[]{:S(2)}) copy-start(f32[1,4608]{1,0:T(1,128)} %param.11) | copy-start | bytes 55300
  271.1 72.6 %all-to-all-start.1 = ((f32[8,36,4608]{2,1,0:T(8,128)}), f32[8,36,4608]{2,1,0:T(8,128)}, u32[]{:S(2)}, u32[]{:S(2)}) async-start(f32[8,36,4608]{2,1,0:T(8,128)} %copy.19), calls=%async_computation.1 | async-start | bytes 11796480 | tf_op jit(solution)/shard_map/all_to_all | solution.py:57
  276.8 83.1 %copy-start.1 = (bf16[1,144,1024]{2,1,0:T(8,128)(2,1)S(1)}, bf16[1,144,1024]{2,1,0:T(8,128)(2,1)}, u32[]{:S(2)}) copy-start(bf16[1,144,1024]{2,1,0:T(8,128)(2,1)} %param.8) | copy-start | bytes 884740
Sparse Core Ops, SparseCore 0:
  13.7 154.2 all-gather.1
where the time goes:
time: 368 us; the launch traced here: 367 us
  waiting for transfers between devices  188 us (51%)
  local copies, waits for them, and re-layouts  102 us (28%)
  matrix products  31.9 us (9%)
  other arithmetic  18 us (5%)
  between operations  14.8 us (4%)
  starting transfers between devices  11.9 us (3%)
    all_gather x1, waiting for transfers between devices, on_device(): lax.all_gather(factor, 'grp', axis=0, tiled=True)  123 us
    all_to_all x1, waiting for transfers between devices, on_device(): lax.all_to_all(bucket, 'front', split_axis=0, concat_axis=0, tiled=True)  64.2 us
    scatter x2, local copies, waits for them, and re-layouts, on_device(): bucket = jnp.zeros((fronts, capacity, col_count), jnp.float32).at[dest_li...  47.1 us
    dot_general x1, matrix products, on_device(): lax.dot_general(factor, lax.all_gather(factor, 'grp', axis=0, tiled=True)...  23.8 us
    scatter x1, local copies, waits for them, and re-layouts, on_device(): row_tags = jnp.full((fronts, capacity), -1.0, jnp.float32).at[dest_live,...  22.1 us
    gather x1, local copies, waits for them, and re-layouts, place_columns(): return jnp.take(rows, source, axis=1) * keep_cols[None, :]  14.1 us
    scatter-add x1, other arithmetic, on_device(): jnp.zeros((row_count, col_count), jnp.float32).at[target_row]  10.6 us
  transfers between devices with their start and end apart: 3, of which 2 were waited for; matrix products, arithmetic and copies ran while one was open for 35% of the time, Pallas kernels for 0%

commit v1 on v0

--- a/solution.py
+++ b/solution.py
@@ -1,7 +1,23 @@
+import functools
 import jax
 import jax.numpy as jnp
 from jax import lax
 from jax.sharding import PartitionSpec as P
+
+
+def remake_values_now(x_part, axis_name):
+    seen = []
+    m = 0
+    n_lanes = lax.axis_size(axis_name)
+    while m < x_part.ndim:
+        seen.append(n_lanes if m == 0 else 1)
+        m = m + 1
+    return lax.all_to_all(
+        jnp.tile(x_part, seen), axis_name, tiled=True, concat_axis=0, split_axis=0
+    )
+
+
+_order_leaves = functools.partial(remake_values_now, axis_name="grp")
 
 
 def place_columns(rows, source, live_count):
@@ -24,7 +40,7 @@
     factor = jnp.dot(panel_f32, inverse_rows.T, precision=highest_precision)
     update = lax.dot_general(
         factor,
-        lax.all_gather(factor, "grp", axis=0, tiled=True),
+        _order_leaves(factor),
         (((1,), (1,)), ((), ())),
         precision=highest_precision,
         preferred_element_type=jnp.float32,

time: 368 us -> 682 us (1.85)
  the two profiles are of different devices: /device:TPU:1 before, /device:TPU:184 now
where the time goes in v1:
time: 682 us; the launch traced here: 680 us
  waiting for transfers between devices  503 us (74%)
  local copies, waits for them, and re-layouts  108 us (16%)
  matrix products  31.1 us (5%)
  starting transfers between devices  18.7 us (3%)
  other arithmetic  18 us (3%)
    all_to_all x1, waiting for transfers between devices, remake_values_now(): lax.all_to_all(jnp.tile(x_part, seen), axis_name, tiled=True, concat_axis...  438 us
    all_to_all x1, waiting for transfers between devices, on_device(): lax.all_to_all(bucket, 'front', split_axis=0, concat_axis=0, tiled=True)  65.1 us
    scatter x2, local copies, waits for them, and re-layouts, on_device(): bucket = jnp.zeros((fronts, capacity, col_count), jnp.float32).at[dest_li...  49.1 us
    dot_general x1, matrix products, on_device(): lax.dot_general(factor, _order_leaves(factor), (((1,), (1,)), ((), ())),...  23.7 us
    scatter x1, local copies, waits for them, and re-layouts, on_device(): row_tags = jnp.full((fronts, capacity), -1.0, jnp.float32).at[dest_live,...  17 us
    gather x1, local copies, waits for them, and re-layouts, place_columns(): return jnp.take(rows, source, axis=1) * keep_cols[None, :]  14.1 us
  transfers between devices with their start and end apart: 3, of which 2 were waited for; matrix products, arithmetic and copies ran while one was open for 19% of the time, Pallas kernels for 0%

profile of v1, /device:TPU:184, one launch (start us, length us, event | category | flops | bytes accessed | tf_op | source)
XLA Modules:
  0.0 680.1 jit_solution(12196984543663282156)
XLA Ops:
  0.6 0.0 copy-start
  0.6 1.0 copy-done
  1.6 4.6 fusion
  6.2 0.0 copy-start.2
  6.2 8.9 %tile.2 = f32[32,144,1024]{2,1,0:T(8,128)} broadcast(f32[144,1024]{1,0:T(8,128)S(1)} %fusion), dimensions={1,2} | broadcast | bytes 19464192 | tf_op jit(solution)/shard_map/tile | solution.py:16
  15.1 0.0 copy-start.5
  15.1 0.0 copy-start.6
  15.1 0.0 copy-start.3
  15.1 9.5 %all-to-all-start = ((f32[32,144,1024]{2,1,0:T(8,128)}), f32[32,144,1024]{2,1,0:T(8,128)}, u32[]{:S(2)}, u32[]{:S(2)}) async-start(f32[32,144,1024]{2,1,0:T(8,128)} %tile.2), calls=%async_computation | async-start | bytes 37748736 | tf_op jit(solution)/shard_map/all_to_all | solution.py:15
  25.3 0.0 copy-done.5
  25.3 0.6 reduce-window.6
  25.9 0.2 slice_reduce_fusion
  26.1 0.0 copy-done.6
  26.1 0.0 copy-done.3
  26.2 0.1 add_bitcast_fusion
  26.3 0.6 broadcast_in_dim.49
  26.9 17.0 %scatter_fusion = f32[8,36]{1,0:T(8,128)} fusion(f32[8,36]{1,0:T(8,128)} %broadcast_in_dim.49, s32[144]{0:T(256)S(1)} %bitcast.40, f32[144]{0:T(256)S(1)} %bitcast.46), kind=kCustom, calls=%fused_computation.1 | custom fusion | bytes 2880 | tf_op jit(solution)/shard_map/scatter | solution.py:64
  43.9 0.1 fusion.6
  44.0 0.1 fusion.7
  44.1 437.6 %all-to-all-done = f32[32,144,1024]{2,1,0:T(8,128)} async-done(((f32[32,144,1024]{2,1,0:T(8,128)}), f32[32,144,1024]{2,1,0:T(8,128)}, u32[]{:S(2)}, u32[]{:S(2)}) %all-to-all-start) | async-done | bytes 18874400 | tf_op jit(solution)/shard_map/all_to_all | solution.py:15
  481.7 4.3 all-to-all-start.1
  486.0 0.0 copy-done.2
  486.0 23.7 %convolution_subtract_fusion = f32[144,4608]{1,0:T(8,128)S(1)} fusion(f32[144,1024]{1,0:T(8,128)S(1)} %fusion, f32[4608,1024]{1,0:T(8,128)} %bitcast.4, f32[1,144,4608]{2,1,0:T(8,128)} %param.9), kind=kOutput, calls=%fused_computation.4 | convolution fusion | flops 8154390528 | bytes 24772608 | tf_op jit(solution)/shard_map/dot_general | solution.py:41
  509.7 3.4 copy.17
  513.1 14.1 %gather_fusion = f32[4608,144]{1,0:T(8,128)} fusion(f32[144,4608]{0,1:T(8,128)} %copy.17, s32[5120]{0:T(1024)S(1)} %pad_clamp_fusion), kind=kCustom, calls=%fused_computation | custom fusion | bytes 5326848 | tf_op jit(solution)/shard_map/jit(_take)/gather | solution.py:25
  527.2 6.4 multiply_bitcast_fusion
  533.7 5.3 copy.18
  538.9 3.0 broadcast_in_dim.53
  541.9 41.0 %scatter_fusion.1 = f32[8,36,4608]{2,0,1:T(8,128)} fusion(f32[8,36,4608]{2,0,1:T(8,128)} %broadcast_in_dim.53, s32[144]{0:T(256)S(1)} %bitcast.41, f32[144,4608]{1,0:T(8,128)} %copy.18), kind=kCustom, calls=%fused_computation.2 | custom fusion | bytes 7963776 | tf_op jit(solution)/shard_map/scatter | solution.py:70
  582.9 8.1 %copy.19 = f32[8,36,4608]{2,1,0:T(8,128)} copy(f32[8,36,4608]{2,0,1:T(8,128)} %scatter_fusion.1) | data formatting | bytes 10616832 | tf_op jit(solution)/shard_map/scatter | solution.py:70
  591.0 0.0 copy-start.4
  591.0 0.0 all-to-all-done.1
  591.0 4.9 all-to-all-start.2
  596.0 0.0 copy-done.4
  596.1 0.1 select_n.81
  596.2 0.0 copy-start.1
  596.2 2.7 fusion.15
  598.9 65.1 %all-to-all-done.2 = f32[8,36,4608]{2,1,0:T(8,128)} async-done(((f32[8,36,4608]{2,1,0:T(8,128)}), f32[8,36,4608]{2,1,0:T(8,128)}, u32[]{:S(2)}, u32[]{:S(2)}) %all-to-all-start.2) | async-done | bytes 5308448 | tf_op jit(solution)/shard_map/all_to_all | solution.py:73
  664.0 5.6 reshape.176
  669.6 10.6 %scatter_custom_fusion.2 = f32[144,4608]{1,0:T(8,128)} fusion(s32[288]{0:T(512)S(1)} %fusion.13, f32[288,4608]{1,0:T(8,128)} %reshape.176, f32[]{:T(128)} %constant.13.clone.1), kind=kCustom, calls=%fused_computation.8 | custom fusion | flops 1327104 | bytes 2654720 | tf_op jit(solution)/shard_map/scatter-add | solution.py:80
  680.1 0.0 copy-done.1
  (16 shorter events, 0.3 us)
Async XLA Ops:
  0.6 1.0 copy-start
  6.2 479.8 %copy-start.2 = (f32[144,1024]{1,0:T(8,128)}, f32[144,1024]{1,0:T(8,128)S(1)}, u32[]{:S(2)}) copy-start(f32[144,1024]{1,0:T(8,128)S(1)} %fusion) | copy-start | bytes 1769476
  15.1 10.1 %copy-start.5 = (s32[1,144,1]{1,2,0:T(1,128)S(1)}, s32[1,144,1]{1,2,0:T(1,128)}, u32[]{:S(2)}) copy-start(s32[1,144,1]{1,2,0:T(1,128)} %param.14) | copy-start | bytes 1732
  15.1 11.0 %copy-start.6 = (s32[1,144]{1,0:T(1,128)S(1)}, s32[1,144]{1,0:T(1,128)}, u32[]{:S(2)}) copy-start(s32[1,144]{1,0:T(1,128)} %param.15) | copy-start | bytes 1732
  15.1 11.0 %copy-start.3 = (s32[1,4608]{1,0:T(1,128)S(1)}, s32[1,4608]{1,0:T(1,128)}, u32[]{:S(2)}) copy-start(s32[1,4608]{1,0:T(1,128)} %param.13) | copy-start | bytes 55300
  15.1 466.6 %all-to-all-start = ((f32[32,144,1024]{2,1,0:T(8,128)}), f32[32,144,1024]{2,1,0:T(8,128)}, u32[]{:S(2)}, u32[]{:S(2)}) async-start(f32[32,144,1024]{2,1,0:T(8,128)} %tile.2), calls=%async_computation | async-start | bytes 37748736 | tf_op jit(solution)/shard_map/all_to_all | solution.py:15
  481.7 109.3 %all-to-all-start.1 = ((f32[8,1,36]{2,1,0:T(1,128)}), f32[8,1,36]{2,1,0:T(1,128)S(1)}, u32[]{:S(2)}, u32[]{:S(2)}) async-start(f32[8,1,36]{2,1,0:T(1,128)} %bitcast.16), calls=%async_computation.1 | async-start | bytes 8192 | tf_op jit(solution)/shard_map/all_to_all | solution.py:74
  591.0 4.9 copy-start.4
  591.0 73.0 %all-to-all-start.2 = ((f32[8,36,4608]{2,1,0:T(8,128)}), f32[8,36,4608]{2,1,0:T(8,128)}, u32[]{:S(2)}, u32[]{:S(2)}) async-start(f32[8,36,4608]{2,1,0:T(8,128)} %copy.19), calls=%async_computation.2 | async-start | bytes 11796480 | tf_op jit(solution)/shard_map/all_to_all | solution.py:73
  596.2 83.9 %copy-start.1 = (bf16[1,144,1024]{2,1,0:T(8,128)(2,1)S(1)}, bf16[1,144,1024]{2,1,0:T(8,128)(2,1)}, u32[]{:S(2)}) copy-start(bf16[1,144,1024]{2,1,0:T(8,128)(2,1)} %param.8) | copy-start | bytes 884740
